TPU v7x, 32 devices: a whole 2x2x4 slice. The times are simulated.
32 devices in a mesh: row: 8 (over y, x, core), col: 4 (over z).
Axes of the slice: x: 2, y: 2, z: 4, core: 2. Of those that a mesh axis runs over, the one named last changes fastest.
Arguments:
- multispectral: float32 [8, 256, 512], P('col', 'row'), may hold values from -6 to 6
- panchromatic: float32 [1024, 2048], P('row', 'col'), may hold values from -6 to 6
- band_gains: float32 [8, 3], replicated, may hold values from 0.5 to 2
Outputs:
- sharpened: float32 [8, 1024, 2048], P(None, 'row', 'col')
All inputs are finite; a program needn't handle non-finite values.
Results may differ from a plain program's by a relative error of at most 0.000065.
Values sent between devices are 32-bit elements; how exact they have to be, the bound alone decides.
No kernel may reach another device: no remote copies, remote signals or barrier semaphores. Data moves between devices by JAX's collectives and lax.ppermute only.
A program may use at most 128 MiB of HBM per device.

v0:
```python
import functools

import jax
import jax.numpy as jnp
import numpy as np
from jax import lax
from jax.experimental import pallas as pl
from jax.experimental.pallas import tpu as pltpu
from jax.sharding import PartitionSpec as P

LEVELS = 3
TAPS = [
    0.2303778133088964,
    0.7148465705529155,
    0.6308807679298587,
    -0.0279837694168599,
    -0.1870348117190931,
    0.0308413818355607,
    0.0328830116668852,
    -0.010597401785069,
]
REACH = 48
COEFS = 24
RIM = 16
NEED = 13
RANK = 21
BAND_ROWS = 56
VMEM = pltpu.VMEM
F32, BF16 = jnp.float32, jnp.bfloat16


def keys_weight(t):
    t = abs(t)
    if t <= 1.0:
        return 1.5 * t**3 - 2.5 * t**2 + 1.0
    return -0.5 * t**3 + 2.5 * t**2 - 4.0 * t + 2.0 if t < 2.0 else 0.0


def upsample_matrix(n):
    m = np.zeros((n, n // 4))
    for y in range(n):
        centre = (y + 0.5) / 4.0 - 0.5
        for k in range(int(np.floor(centre)) - 1, int(np.floor(centre)) + 3):
            m[y, k % (n // 4)] += keys_weight(centre - k)
    return m


def low_matrix(n, tree):
    taps, offset = (TAPS, 3) if tree == 0 else (TAPS[::-1], 4)
    m = np.zeros((n // 2, n))
    for k in range(n // 2):
        for j in range(8):
            m[k, (2 * k + j - offset) % n] += taps[j]
    return m


@functools.lru_cache(None)
def smooth_matrix(n, level):
    total = 0.0
    for tree in range(2):
        chain = np.eye(n)
        for step in range(level):
            chain = low_matrix(n >> step, tree) @ chain
        total = total + 0.5 * chain.T @ chain
    return total


def split_const(m):
    m = np.asarray(m, np.float32)
    hi = m.astype(BF16)
    lo = (m - hi.astype(np.float32)).astype(BF16)
    return hi, lo


@functools.lru_cache(None)
def constants(rows, cols):
    half = cols // 2
    n = 1024
    q = [smooth_matrix(n, level) for level in (1, 2, 3)]
    o = 256
    stack = lambda lo, hi: np.concatenate([m[o : o + 128, lo:hi] for m in q])
    send, recv = [], []
    for lo, hi in ((o - REACH, o), (o + 128, o + 128 + REACH)):
        _, s, vt = np.linalg.svd(stack(lo, hi), full_matrices=False)
        assert s[COEFS - 3] < 1e-14
        send.append(vt[:COEFS])
        recv.append(vt[:COEFS].T)
    below, above = send[0], send[1]
    own, edge = [], ([], [])
    for m in q:
        body = m[o : o + rows]
        own.append(body[:, o : o + rows])
        edge[0].append(body[:REACH, o - REACH : o] @ recv[0])
        edge[1].append(body[-REACH:, o + rows : o + rows + REACH] @ recv[1])
    c1, c2 = [], []
    for m in q:
        body = m[o : o + half]
        c1.append(body[:, o : o + half].T)
        left, right = body[:, o - REACH : o], body[:, o + half : o + half + REACH]
        nothing = np.zeros((half, COEFS))
        first = np.concatenate([left @ recv[0], nothing, right], 1).T
        second = np.concatenate([nothing, right @ recv[1], left], 1).T
        c2.append((first, second))
    qu = q[2] @ upsample_matrix(n)
    p = o // 4
    low = rows // 4
    cu = np.concatenate(
        [
            qu[o : o + cols, p : p + cols // 4],
            qu[o : o + cols, p - RIM : p],
            qu[o : o + cols, p + cols // 4 : p + cols // 4 + RIM],
        ],
        1,
    ).T
    ru = qu[o : o + rows]
    ru_own, ru_rims = ru[:, p : p + low], (ru[:, p - RIM : p], ru[:, p + low : p + low + RIM])
    ru_ends = (ru_rims[0][:BAND_ROWS], ru_rims[1][rows - BAND_ROWS :])
    assert not ru_rims[0][BAND_ROWS:].any() and not ru_rims[1][: rows - BAND_ROWS].any()

    def three(m):
        hi, lo = split_const(m)
        return np.concatenate([hi, hi, lo], 1)

    pair = lambda m: np.concatenate(split_const(m), 1)
    parts = dict(below=pair(below), above=pair(above))
    for level in range(LEVELS):
        parts[f"own{level}"] = pair(own[level])
    for level in range(LEVELS):
        parts[f"c1{level}hi"], parts[f"c1{level}lo"] = split_const(c1[level])
    nothing = np.zeros((REACH, COEFS))
    for level in range(LEVELS):
        parts[f"edge{level}"] = three(np.block([[edge[0][level], nothing], [nothing, edge[1][level]]]))
    for side in range(2):
        parts[f"ru{side}"] = three(np.concatenate([ru_own, ru_rims[side]], 1))
    for side in range(2):
        assert not (ru_rims[0][:, : RIM - NEED] if side == 0 else ru_rims[1][:, NEED:]).any()
        used = ru_ends[side][:, RIM - NEED :] if side == 0 else ru_ends[side][:, :NEED]
        parts[f"end{side}"] = three(np.pad(used, ((0, 0), (0, RIM - NEED))))
        gap = np.zeros((BAND_ROWS - REACH, LEVELS * COEFS))
        m = np.concatenate(edge[side], 1)
        m = np.concatenate([m, gap] if side == 0 else [gap, m])
        for name, x in zip(("fixhi", "fixlo"), split_const(m)):
            parts[f"{name}{side}"] = np.concatenate([x] * 3, 1)
    for level in range(LEVELS):
        for h in range(2):
            parts[f"c2{level}{h}hi"], parts[f"c2{level}{h}lo"] = split_const(c2[level][h])
    for h in range(2):
        parts[f"cu{h}hi"], parts[f"cu{h}lo"] = split_const(cu[:, h * half : (h + 1) * half])
    table, where, at = [], {}, 0
    for name, m in parts.items():
        high = -(-m.shape[0] // 16) * 16
        table.append(np.pad(np.asarray(m, np.float32), ((0, high - m.shape[0]), (0, half - m.shape[1]))))
        where[name] = (at, m.shape)
        at += high
    table = np.concatenate(table).astype(BF16)
    return table, (where["own0"][0], where["edge0"][0]), where


class Table:
    def __init__(self, ref, where):
        self.ref, self.where = ref, where

    def __getitem__(self, name):
        at, (high, wide) = self.where[name]
        return self.ref[at : at + high, 0:wide]

    def pair(self, name):
        x = self[name]
        wide = x.shape[1] // 2
        return x[:, :wide], x[:, wide:]

    def side(self, name, below):
        (first, (high, wide)), (second, _) = self.where[name + "0"], self.where[name + "1"]
        at = pl.multiple_of(jnp.where(below, second, first), 16)
        return self.ref[pl.ds(at, high), 0:wide]

    def two(self, name):
        return self[name + "hi"], self[name + "lo"]


def swap_pairs(count):
    return [(i, i ^ 1) for i in range(count)]


def odd_pairs(count):
    return [(i, (i - 1) % count if i % 2 == 0 else (i + 1) % count) for i in range(count)]


def column_steps(count):
    if count == 4:
        return [
            ([(i, i ^ k) for i in range(4)], k != 2, lambda c, k=k: c ^ k, lambda c, k=k: c ^ k)
            for k in (1, 3, 2)
        ]
    return [
        (
            [(i, (i + k) % count) for i in range(count)],
            k in (1, count - 1),
            lambda c, k=k: lax.rem(c + k, count),
            lambda c, k=k: lax.rem(c + count - k, count),
        )
        for k in [1, count - 1] + list(range(2, count - 1))
    ]


def split(x):
    hi = x.astype(BF16)
    return hi, (x - hi.astype(F32)).astype(BF16)


def dot(a, b, dims=((1,), (0,))):
    return lax.dot_general(a, b, (dims, ((), ())), preferred_element_type=F32)


def dot3(a, b, dims=((1,), (0,))):
    return dot(a[0], b[0], dims) + dot(a[1], b[0], dims) + dot(a[0], b[1], dims)


def rows3(a, b):
    high = a[0].shape[0]
    both = dot(jnp.concatenate(a, 0), b[0])
    return both[:high] + both[high:] + dot(a[0], b[1])


def three_high(x):
    if x.shape[0] % 16:
        hi = x.astype(BF16).astype(F32)
        return jnp.concatenate([hi, x - hi, hi], 0).astype(BF16)
    hi, lo = split(x)
    return jnp.concatenate([hi, lo, hi], 0)


def lanes(shape):
    return lax.broadcasted_iota(jnp.int32, shape, 1)


def pack_chunk(out, ms_ref, to, count):
    bands, low = ms_ref.shape[0], ms_ref.shape[1]
    main = bands * low
    block = lambda k: pl.ds(pl.multiple_of(lax.rem(k + count, count) * 128, 128), 128)
    packed = None
    for i in range(bands):
        out[i * low : (i + 1) * low, :] = ms_ref[i, :, block(to)]
        left, right = ms_ref[i, :, block(to - 1)], ms_ref[i, :, block(to + 1)]
        rim = jnp.where(lanes(left.shape) >= 64, left, right)
        for g in range(low // RIM):
            slot = i * (low // RIM) + g
            rolled = pltpu.roll(rim[g * RIM : (g + 1) * RIM], (2 * RIM * slot + RIM) % 128, 1)
            packed = rolled if slot == 0 else jnp.where(lanes(rolled.shape) >= 2 * RIM * slot, rolled, packed)
    out[main : main + RIM, :] = packed


def pack_kernel(count, where, ms_ref, pan_ref, table_ref, *out_refs):
    c, r = lax.axis_index("col"), lax.axis_index("row")
    table = Table(table_ref, where)
    main = ms_ref.shape[0] * ms_ref.shape[1]
    rows, cols = pan_ref.shape
    below, above = table.pair("below"), table.pair("above")
    choose = lambda first: tuple(
        jnp.where(first, x.astype(F32), y.astype(F32)).astype(BF16) for x, y in zip(below, above)
    )
    for step, out in zip(column_steps(count), out_refs):
        to = step[2](c)
        pack_chunk(out, ms_ref, to, count)
        if step[1]:
            to_right = to == lax.rem(c + 1, count)
            edge = jnp.where(to_right, pltpu.roll(pan_ref[:, cols - 128 :], REACH, 1), pan_ref[:, :128])
            out[main + RIM : main + RIM + COEFS, :] = dot3(choose(to_right), split(edge[:, :REACH]), ((1,), (1,)))
    bottom = lax.rem(r, 2) == 1
    at = pl.multiple_of(jnp.where(bottom, rows - REACH, 0), 16)
    full = dot3(choose(bottom), split(pan_ref[pl.ds(at, REACH), :]))
    for k in range(cols // 128):
        out_refs[-1][k * COEFS : (k + 1) * COEFS, :] = full[:, k * 128 : (k + 1) * 128]


def stage_kernel(count, where, cuts, *refs):
    ms_hbm, pan_hbm, table_hbm = refs[:3]
    own_ref, top_ref, bot_ref, pan_ref, table_ref, e1, ms_ref, sems = refs[3:]
    ends = (0,) + cuts + (table_ref.shape[0],)
    parts = [pl.ds(x, y - x) for x, y in zip(ends, ends[1:])]
    moves = [(pan_hbm, pan_ref)] + [(table_hbm.at[x], table_ref.at[x]) for x in parts[:2]]
    moves += [(ms_hbm, ms_ref), (table_hbm.at[parts[2]], table_ref.at[parts[2]])]
    copies = [pltpu.make_async_copy(x, y, sems.at[k]) for k, (x, y) in enumerate(moves)]
    for copy in copies:
        copy.start()
    copies[0].wait()
    copies[1].wait()
    table = Table(table_ref, where)
    rows, cols = pan_ref.shape
    half = cols // 2
    for out, name, at in ((bot_ref, "below", rows - REACH), (top_ref, "above", 0)):
        full = dot3(table.pair(name), split(pan_ref[at : at + REACH, :]))
        for k in range(cols // 128):
            out[k * COEFS : (k + 1) * COEFS, :] = full[:, k * 128 : (k + 1) * 128]
    copies[2].wait()
    hi, lo = split(pan_ref[...])
    both = jnp.concatenate([hi, lo], 0)
    for level in range(LEVELS):
        t = dot(jnp.concatenate([table.pair(f"own{level}")[0]] * 2, 1), both) + dot(table.pair(f"own{level}")[1], hi)
        main = rows3(split(jnp.concatenate([t[:, :half], t[:, half:]], 0)), table.two(f"c1{level}"))
        e1[level, :, 0:half] = main[:rows]
        e1[level, :, half:] = main[rows:]
    copies[3].wait()
    pack_chunk(own_ref, ms_ref, lax.axis_index("col"), count)
    copies[4].wait()


def rim_kernel(count, low, where, top_ref, bot_ref, table_ref, *refs):
    table = Table(table_ref, where)
    q = refs[:count]
    a_ref, b_ref, xh_ref = refs[count:]
    c, r = lax.axis_index("col"), lax.axis_index("row")
    steps = column_steps(count)
    bands = (q[0].shape[0] - RIM) // low
    main = bands * low
    even = lax.rem(r, 2) == 0
    first = q[1][main + RIM : main + RIM + COEFS, :]
    second = q[2][main + RIM : main + RIM + COEFS, :]
    first_is_right = steps[0][3](c) == lax.rem(c + 1, count)
    left = jnp.where(first_is_right, second, first)
    right = jnp.where(first_is_right, first, second)
    filler = jnp.zeros((128 - 2 * COEFS, 128), F32)
    xh = jnp.concatenate([left, right, filler], 0).T
    xh_ref[...] = xh
    per = low // RIM
    total = count * bands

    def fill(out, bottom, far):
        height = 0 if far else top_ref.shape[0]
        if not far:
            out[0:height, :] = (bot_ref if bottom else top_ref)[...]
        v = table.pair("below" if bottom else "above")
        corner = dot3(v, split(xh[xh.shape[0] - REACH :] if bottom else xh[:REACH]))
        if far:
            tight = jnp.where(lanes(corner.shape) < RANK, corner, pltpu.roll(corner, 128 - (COEFS - RANK), 1))
            packed = tight[0:8]
            for g in (1, 2):
                turned = pltpu.roll(tight[8 * g : 8 * g + 8], 2 * RANK * g, 1)
                packed = jnp.where(lanes(packed.shape) >= 2 * RANK * g, turned, packed)
            out[height : height + 8, :] = packed
        else:
            out[height : height + COEFS, :] = corner
        base = height + (8 if far else COEFS)
        rim_rows = NEED if far else RIM
        packed = None
        for n in range(total):
            ref, i = q[n // bands], n % bands
            row = (i + 1) * low - rim_rows if bottom else i * low
            out[base + n * rim_rows : base + (n + 1) * rim_rows, :] = ref[row : row + rim_rows, :]
            slot = per * (i + 1) - 1 if bottom else per * i
            rim = pltpu.roll(ref[main : main + RIM, :], (2 * RIM * (n % 4 - slot)) % 128, 1)
            packed = rim if n % 4 == 0 else jnp.where(lanes(rim.shape) >= 2 * RIM * (n % 4), rim, packed)
            if n % 4 == 3 or n == total - 1:
                spot = base + total * rim_rows + (n // 4) * rim_rows
                out[spot : spot + rim_rows, :] = packed[RIM - rim_rows :] if bottom else packed[:rim_rows]

    @pl.when(even)
    def _():
        fill(a_ref, 1, False)
        fill(b_ref, 0, True)

    @pl.when(jnp.logical_not(even))
    def _():
        fill(a_ref, 0, False)
        fill(b_ref, 1, True)


def own_rims(own_right, own_left, xh):
    inner = lanes(xh.shape) < 2 * COEFS
    return (
        jnp.where(inner, xh, pltpu.roll(own_right, 2 * COEFS, 1)),
        jnp.where(inner, xh, pltpu.roll(own_left, 2 * COEFS + REACH, 1)),
    )


def columns(x, cols, table, level):
    half = cols // 2
    high = x.shape[0]
    wide = 2 * COEFS + REACH
    main = rows3(split(jnp.concatenate([x[:, :half], x[:, half:cols]], 0)), table.two(f"c1{level}"))
    out = []
    for h in range(2):
        rim = split(x[:, cols + h * 128 : cols + h * 128 + wide])
        product = dot3 if high % 16 else rows3
        out.append(main[h * high : (h + 1) * high] + product(rim, table.two(f"c2{level}{h}")))
    return out


def low_columns(x_ref, y_ref, table):
    x = split(x_ref[:, 0 : 128 + 2 * RIM])
    half = y_ref.shape[1] // 2
    for h in range(2):
        y_ref[:, h * half : (h + 1) * half] = rows3(x, table.two(f"cu{h}"))


def fill_rows(xe, at, cols, piece, xh):
    blocks = cols // 128
    for k in range(blocks):
        xe[at, k * 128 : (k + 1) * 128] = piece(k)
    f, s = own_rims(piece(blocks // 2), piece(blocks // 2 - 1), xh)
    xe[at, cols : cols + 128] = f
    xe[at, cols + 128 : cols + 256] = s


def coef_piece(ref):
    return lambda k: ref[k * COEFS : (k + 1) * COEFS, :]


def band_rims(mext, ref, total, base, high, skip, rim_rows=RIM):
    filler = [jnp.zeros((RIM - rim_rows, 128), F32)] if rim_rows < RIM else []
    whole = lambda x: jnp.concatenate([x] + filler, 0) if filler else x
    for n in range(total):
        at = slice(n * high + skip, n * high + skip + RIM)
        mext[at, 0:128] = whole(ref[base + n * rim_rows : base + (n + 1) * rim_rows, :])
        spot = base + total * rim_rows + (n // 4) * rim_rows
        mext[at, 128:256] = pltpu.roll(whole(ref[spot : spot + rim_rows, :]), (-2 * RIM * (n % 4)) % 128, 1)


def local_kernel(count, low, where, gains_ref, *refs):
    q, refs = refs[:count], refs[count:]
    pan_ref, xh_ref, a_ref, far_ref, e1, table_ref = refs[:6]
    part_ref, fix_ref, xr, xe, e3, mext, y_ref = refs[6:]
    table = Table(table_ref, where)
    c, r = lax.axis_index("col"), lax.axis_index("row")
    below = lax.rem(r, 2) == 0
    steps = column_steps(count)
    bands = (q[0].shape[0] - RIM) // low
    total = count * bands
    main = bands * low
    rows, cols = pan_ref.shape
    half = cols // 2
    per = low // RIM
    high = low + RIM
    for n in range(total):
        ref, i = q[n // bands], n % bands
        mext[n * high : n * high + low, 0:128] = ref[i * low : (i + 1) * low, :]
        for g in range(per):
            at = n * high + g * RIM
            mext[at : at + RIM, 128:256] = pltpu.roll(
                ref[main : main + RIM, :], (-2 * RIM * (i * per + g)) % 128, 1
            )
    band_rims(mext, a_ref, total, (cols // 128 + 1) * COEFS, high, low)
    low_columns(mext, y_ref, table)
    xr[:, 0:128], xr[:, 128:256] = own_rims(
        pan_ref[:, half : half + 128], pan_ref[:, half - 128 : half], xh_ref[...]
    )
    blocks = cols // 128
    at = lambda under: pl.ds(pl.multiple_of(jnp.where(under, COEFS, 0), 8), COEFS)
    fill_rows(xe, at(below), cols, coef_piece(a_ref), a_ref[blocks * COEFS : (blocks + 1) * COEFS, :])
    fill_rows(xe, at(jnp.logical_not(below)), cols, coef_piece(far_ref), jnp.zeros((COEFS, 128), F32))
    hi, lo = split(xr[...])
    both = jnp.concatenate([hi, lo], 0)
    wide = 2 * COEFS + REACH
    x = xe[...]
    before = [pan_ref[:, h * half : (h + 1) * half] for h in range(2)]
    for level in range(LEVELS):
        ohi, olo = table.pair(f"own{level}")
        t = dot(jnp.concatenate([ohi, ohi], 1), both) + dot(olo, hi)
        for h, z in enumerate(columns(x, cols, table, level)):
            hs = slice(h * half, (h + 1) * half)
            de = dot(table[f"edge{level}"], three_high(z))
            e = e1[level, :, hs] + rows3(split(t[:, h * 128 : h * 128 + wide]), table.two(f"c2{level}{h}"))
            e = jnp.concatenate([e[:REACH] + de[:REACH], e[REACH : rows - REACH], e[rows - REACH :] + de[REACH:]], 0)
            e3[level, :, hs] = before[h] - e
            before[h] = e
    far_below = jnp.logical_not(below)
    fix = table.side("fixhi", far_below).astype(F32) + table.side("fixlo", far_below).astype(F32)
    lane = lanes((1, fix.shape[1]))
    level_of = lax.rem(lane, LEVELS * COEFS) // COEFS
    first_two = lanes(fix.shape) < 2 * LEVELS * COEFS
    for j in range(count):
        src = c if j == 0 else steps[j - 1][3](c)
        for i in range(bands):
            n = j * bands + i
            band = src * bands + i
            g1, g2, g3 = gains_ref[0, band], gains_ref[1, band], gains_ref[2, band]
            factor = jnp.where(level_of == 0, g2 - g1, jnp.where(level_of == 1, g3 - g2, -g3))
            scaled = factor * fix
            hi = scaled.astype(BF16).astype(F32)
            fix_ref[n * BAND_ROWS : (n + 1) * BAND_ROWS, :] = jnp.where(first_two, hi, scaled - hi)
            part_ref[n] = (
                dot(table.side("ru", below), three_high(y_ref[n * high : (n + 1) * high, :]))
                + g1 * e3[0]
                + g2 * e3[1]
                + g3 * e3[2]
            )


def main_kernel(count, bands, where, *refs):
    part_ref, fix_ref, b_ref, table_ref, out_ref, mext, y_ref, obuf, sems = refs
    table = Table(table_ref, where)
    c, r = lax.axis_index("col"), lax.axis_index("row")
    steps = column_steps(count)
    below = lax.rem(r, 2) == 1
    total, rows, cols = part_ref.shape
    half = cols // 2
    source = [c if j == 0 else steps[j - 1][3](c) for j in range(count)]
    band = [source[n // bands] * bands + n % bands for n in range(total)]
    done = pl.ds(pl.multiple_of(jnp.where(below, 0, BAND_ROWS), 8), rows - BAND_ROWS)
    late = pl.ds(pl.multiple_of(jnp.where(below, rows - BAND_ROWS, 0), 8), BAND_ROWS)
    copies = [
        pltpu.make_async_copy(part_ref.at[n, done], out_ref.at[band[n], done], sems.at[0, n])
        for n in range(total)
    ]

    @pl.loop(0, total)
    def _(k):
        at = sum(jnp.where(k == n, band[n], 0) for n in range(total))
        pltpu.make_async_copy(part_ref.at[k, done], out_ref.at[at, done], sems.at[0, k]).start()

    band_rims(mext, b_ref, total, 8, RIM, 0, NEED)
    low_columns(mext, y_ref, table)
    packed = b_ref[0:8, :]
    tight = jnp.concatenate([pltpu.roll(packed, (-2 * RANK * g) % 128, 1) for g in range(3)], 0)
    corner = jnp.where(lanes(tight.shape) < COEFS, tight, pltpu.roll(tight, COEFS - RANK, 1))
    corner = split(corner[:, : 2 * COEFS])
    ends = []
    for h in range(2):
        lane = slice(0, 128) if h == 0 else slice(half - 128, half)
        rim = tuple(
            jnp.concatenate([table.two(f"c2{level}{h}")[k][: 2 * COEFS, lane] for level in range(LEVELS)], 1)
            for k in range(2)
        )
        ends.append(dot3(corner, rim))
    stacked = [jnp.concatenate([z[:, level * 128 : (level + 1) * 128] for z in ends], 1) for level in range(LEVELS)]
    fix = dot(fix_ref[...].astype(BF16), three_high(jnp.concatenate(stacked, 0)))
    for n in range(total):
        rim = three_high(y_ref[n * RIM : (n + 1) * RIM, :])
        base = part_ref[n, late, :] + dot(table.side("end", below), rim)
        add = fix[n * BAND_ROWS : (n + 1) * BAND_ROWS]
        obuf[n, :, 0:128] = base[:, 0:128] + add[:, 0:128]
        obuf[n, :, 128 : cols - 128] = base[:, 128 : cols - 128]
        obuf[n, :, cols - 128 :] = base[:, cols - 128 :] + add[:, 128:]
        copy = pltpu.make_async_copy(obuf.at[n], out_ref.at[band[n], late], sems.at[1, n])
        copy.start()
        copies.append(copy)
    for copy in copies:
        copy.wait()


def on_device(multispectral, panchromatic, band_gains):
    count, row_count = lax.axis_size("col"), lax.axis_size("row")
    bands, low, _ = multispectral.shape
    rows, cols = panchromatic.shape
    total = count * bands
    table, cuts, where = constants(rows, cols)
    small = table[: cuts[0]]
    steps = column_steps(count)
    chunk = bands * low + RIM
    shape = lambda n, m=128: jax.ShapeDtypeStruct((n, m), F32)
    whole = pl.BlockSpec(memory_space=VMEM)
    heights = [chunk + (COEFS if step[1] else 0) for step in steps]
    height = cols // 128 * COEFS
    in_hbm = lambda *xs: [pltpu.with_memory_space_constraint(x, pltpu.HBM) for x in xs]
    *packed, far = pl.pallas_call(
        functools.partial(pack_kernel, count, where),
        out_shape=[VMEM((h, 128), F32) for h in heights + [height]],
        grid=(1,),
        in_specs=[
            pl.BlockSpec(multispectral.shape, lambda i: (0, 0, 0)),
            pl.BlockSpec(panchromatic.shape, lambda i: (0, 0)),
            pl.BlockSpec(small.shape, lambda i: (0, 0)),
        ],
        out_specs=[whole] * (len(heights) + 1),
        compiler_params=pltpu.CompilerParams(vmem_limit_bytes=8 << 20),
        name="pack",
    )(*in_hbm(multispectral, panchromatic, jnp.asarray(small)))
    params = lambda mib: pltpu.CompilerParams(vmem_limit_bytes=mib << 20)
    cost = lambda flops: pl.CostEstimate(flops=flops, bytes_accessed=10**6, transcendentals=0)
    table = jnp.asarray(table)
    own, top, bot, pan, table, e1 = pl.pallas_call(
        functools.partial(stage_kernel, count, where, cuts),
        out_shape=[
            VMEM((chunk, 128), F32),
            VMEM((height, 128), F32),
            VMEM((height, 128), F32),
            VMEM((rows, cols), F32),
            VMEM(table.shape, BF16),
            VMEM((LEVELS, rows, cols), F32),
        ],
        in_specs=[pl.BlockSpec(memory_space=pltpu.HBM)] * 3,
        out_specs=[whole] * 6,
        scratch_shapes=[VMEM(multispectral.shape, F32), pltpu.SemaphoreType.DMA((5,))],
        compiler_params=params(8),
        cost_estimate=cost(10**9),
        name="stage",
    )(*in_hbm(multispectral, panchromatic, table))
    q = [own]
    for x, step in zip(packed, steps):
        q.append(lax.ppermute(x, "col", step[0]))
    far = lax.ppermute(far, "row", odd_pairs(row_count))
    sent = lambda corner, rim: -(-(corner + total * rim + -(-total // 4) * rim) // 8) * 8
    a, b, xh = pl.pallas_call(
        functools.partial(rim_kernel, count, low, where),
        out_shape=[shape(height + sent(COEFS, RIM)), shape(sent(8, NEED)), shape(rows)],
        in_specs=[whole] * (3 + count),
        out_specs=[whole] * 3,
        compiler_params=params(8),
        name="rim",
    )(top, bot, table, *q)
    a = lax.ppermute(a, "row", swap_pairs(row_count))
    b = lax.ppermute(b, "row", odd_pairs(row_count))
    smem = pl.BlockSpec(memory_space=pltpu.SMEM)
    part, scaled = pl.pallas_call(
        functools.partial(local_kernel, count, low, where),
        out_shape=[
            jax.ShapeDtypeStruct((total, rows, cols), F32),
            shape(total * BAND_ROWS, 3 * LEVELS * COEFS),
        ],
        in_specs=[smem] + [whole] * (count + 6),
        out_specs=[whole] * 2,
        scratch_shapes=[
            VMEM((rows, 256), F32),
            VMEM((2 * COEFS, cols + 256), F32),
            VMEM((LEVELS, rows, cols), F32),
            VMEM((total * (low + RIM), 256), F32),
            VMEM((total * (low + RIM), cols), F32),
        ],
        compiler_params=params(16),
        cost_estimate=cost(4 * 10**9),
        name="local",
    )(band_gains.T, *q, pan, xh, a, far, pltpu.with_memory_space_constraint(e1, VMEM), table)
    return pl.pallas_call(
        functools.partial(main_kernel, count, bands, where),
        out_shape=jax.ShapeDtypeStruct((total, rows, cols), F32),
        in_specs=[whole] * 4,
        out_specs=pl.BlockSpec(memory_space=pltpu.HBM),
        scratch_shapes=[
            VMEM((total * RIM, 256), F32),
            VMEM((total * RIM, cols), F32),
            VMEM((total, BAND_ROWS, cols), F32),
            pltpu.SemaphoreType.DMA((2, total)),
        ],
        compiler_params=params(16),
        name="combine",
    )(part, scaled, b, table)


def solution(mesh):
    in_specs = (P("col", "row", None), P("row", "col"), P())
    out_specs = P(None, "row", "col")
    return jax.shard_map(
        on_device, mesh=mesh, in_specs=in_specs, out_specs=out_specs, check_vma=False
    )
```

profile of v0, /device:TPU:0, one launch (start us, length us, event | category | flops | bytes accessed | tf_op | source)
XLA Modules:
  0.0 22.3 jit_solution(2671261075197956200)
XLA Ops:
  0.0 1.3 %pack.1 = (f32[104,128]{1,0:T(8,128)S(1)}, f32[104,128]{1,0:T(8,128)S(1)}, f32[80,128]{1,0:T(8,128)S(1)}, f32[96,128]{1,0:T(8,128)S(1)}) custom-call(f32[2,32,512]{2,1,0:T(8,128)} %ms_ref.1, f32[128,512]{1,0:T(8,128)} %pan_ref.1, bf16[64,256]{1,0:T(8,128)(2,1)} %constant.4.clone.table_ref), custom_call_target="tpu_custom_call" | custom-call | tf_op jit(solution)/shard_map/pack/pallas_call | solution.py:555
  1.3 4.1 %collective-permute-start.2 = (f32[80,128]{1,0:T(8,128)S(1)}, f32[80,128]{1,0:T(8,128)S(1)}, u32[]{:S(2)}, u32[]{:S(2)}) collective-permute-start(f32[80,128]{1,0:T(8,128)S(1)} %get-tuple-element.23), channel_id=1, source_target_pairs={{0,2},{1,3},{2,0},{3,1},{4,6},{5,7},{6,4},{7,5},{8,10},{9,11},{10,... | collective-permute-start | bytes 122888 | tf_op jit(solution)/shard_map/ppermute | solution.py:590
  5.4 1.6 %collective-permute-start = (f32[104,128]{1,0:T(8,128)S(1)}, f32[104,128]{1,0:T(8,128)S(1)}, u32[]{:S(2)}, u32[]{:S(2)}) collective-permute-start(f32[104,128]{1,0:T(8,128)S(1)} %get-tuple-element.21), channel_id=1, source_target_pairs={{0,1},{1,0},{2,3},{3,2},{4,5},{5,4},{6,7},{7,6},{8,9},{9,8},{10,11... | collective-permute-start | bytes 159752 | tf_op jit(solution)/shard_map/ppermute | solution.py:590
  7.0 0.0 copy-start
  7.0 0.0 collective-permute-start.1
  7.0 2.3 %stage.1 = (f32[80,128]{1,0:T(8,128)S(1)}, f32[96,128]{1,0:T(8,128)S(1)}, f32[96,128]{1,0:T(8,128)S(1)}, f32[128,512]{1,0:T(8,128)S(1)}, bf16[4704,256]{1,0:T(8,128)(2,1)S(1)}, /*index=5*/f32[3,128,512]{2,1,0:T(8,128)S(1)}) custom-call(f32[2,32,512]{2,1,0:T(8,128)} %ms_ref.1, f32[128,512]{1,0:T(8,128)} %pan_ref.1, bf16[4704,256]{1,0:T(8,128)(2,1)} %constant.5.clone.refs_2_), custom_call_target="tpu_custom_call" | custom-call | flops 1000000000 | bytes 1000000 | tf_op jit(solution)/shard_map/stage/pallas_call | solution.py:571
  9.3 0.0 collective-permute-done.2.refs_3_
  9.3 0.2 %collective-permute-done.refs_1_ = f32[104,128]{1,0:T(8,128)S(1)} collective-permute-done((f32[104,128]{1,0:T(8,128)S(1)}, f32[104,128]{1,0:T(8,128)S(1)}, u32[]{:S(2)}, u32[]{:S(2)}) %collective-permute-start) | collective-permute-done | bytes 53280 | tf_op jit(solution)/shard_map/ppermute | solution.py:590
  9.5 3.4 %collective-permute-done.1.refs_2_ = f32[104,128]{1,0:T(8,128)S(1)} collective-permute-done((f32[104,128]{1,0:T(8,128)S(1)}, f32[104,128]{1,0:T(8,128)S(1)}, u32[]{:S(2)}, u32[]{:S(2)}) %collective-permute-start.1) | collective-permute-done | bytes 53280 | tf_op jit(solution)/shard_map/ppermute | solution.py:590
  12.9 0.4 %rim.1 = (f32[280,128]{1,0:T(8,128)S(1)}, f32[144,128]{1,0:T(8,128)S(1)}, f32[128,128]{1,0:T(8,128)S(1)}) custom-call(f32[96,128]{1,0:T(8,128)S(1)} %get-tuple-element.25.top_ref, f32[96,128]{1,0:T(8,128)S(1)} %get-tuple-element.26.bot_ref, bf16[4704,256]{1,0:T(8,128)(2,1)S(1)} %get-tuple-element.27.table_ref.refs_9_.refs_3_, ...), custom_call_target="tpu_custom_call" | custom-call | tf_op jit(solution)/shard_map/rim/pallas_call | solution.py:593
  13.3 0.0 collective-permute-start.3
  13.4 2.5 %collective-permute-start.4 = (f32[96,128]{1,0:T(8,128)S(1)}, f32[96,128]{1,0:T(8,128)S(1)}, u32[]{:S(2)}, u32[]{:S(2)}) collective-permute-start(f32[96,128]{1,0:T(8,128)S(1)} %get-tuple-element.30), channel_id=1, source_target_pairs={{0,28},{4,8},{8,4},{12,16},{16,12},{20,24},{24,20},{28,0},{1,29},{... | collective-permute-start | bytes 147464 | tf_op jit(solution)/shard_map/ppermute | solution.py:591
  15.9 0.2 collective-permute-start.5
  16.1 1.8 %collective-permute-done.4.refs_7_ = f32[96,128]{1,0:T(8,128)S(1)} collective-permute-done((f32[96,128]{1,0:T(8,128)S(1)}, f32[96,128]{1,0:T(8,128)S(1)}, u32[]{:S(2)}, u32[]{:S(2)}) %collective-permute-start.4) | collective-permute-done | bytes 49184 | tf_op jit(solution)/shard_map/ppermute | solution.py:591
  17.8 0.0 collective-permute-done.3.refs_6_
  17.8 0.0 copy-done
  17.9 2.7 %local.1 = (f32[8,128,512]{2,1,0:T(8,128)S(1)}, f32[448,216]{1,0:T(8,128)S(1)}) custom-call(f32[3,8]{1,0:T(4,128)S(1)} %bitcast.1, f32[80,128]{1,0:T(8,128)S(1)} %get-tuple-element.20.refs_0_, f32[104,128]{1,0:T(8,128)S(1)} %collective-permute-done.refs_1_, f32[104,128]{1,0:T(8,128)S(1)} %collective-permute-done.1.refs_2_, ...), custom_call_target="tpu_custom_call" | custom-call | flops 4000000000 | bytes 1000000 | tf_op jit(solution)/shard_map/local/pallas_call | solution.py:604
  20.6 0.1 collective-permute-done.5.refs_2_
  20.7 1.6 %combine.1 = f32[8,128,512]{2,1,0:T(8,128)} custom-call(f32[8,128,512]{2,1,0:T(8,128)S(1)} %get-tuple-element.32.refs_0_, f32[448,216]{1,0:T(8,128)S(1)} %get-tuple-element.33.refs_1_, f32[144,128]{1,0:T(8,128)S(1)} %collective-permute-done.5.refs_2_, bf16[4704,256]{1,0:T(8,128)(2,1)S(1)} %get-tuple-element.27.table_ref.refs_9_.refs_3_), custom_call_target="tpu_custom_call" | custom-call | tf_op jit(solution)/shard_map/combine/pallas_call | solution.py:623
Async XLA Ops:
  1.3 8.0 %collective-permute-start.2 = (f32[80,128]{1,0:T(8,128)S(1)}, f32[80,128]{1,0:T(8,128)S(1)}, u32[]{:S(2)}, u32[]{:S(2)}) collective-permute-start(f32[80,128]{1,0:T(8,128)S(1)} %get-tuple-element.23), channel_id=1, source_target_pairs={{0,2},{1,3},{2,0},{3,1},{4,6},{5,7},{6,4},{7,5},{8,10},{9,11},{10,... | collective-permute-start | bytes 122888 | tf_op jit(solution)/shard_map/ppermute | solution.py:590
  5.4 4.1 %collective-permute-start = (f32[104,128]{1,0:T(8,128)S(1)}, f32[104,128]{1,0:T(8,128)S(1)}, u32[]{:S(2)}, u32[]{:S(2)}) collective-permute-start(f32[104,128]{1,0:T(8,128)S(1)} %get-tuple-element.21), channel_id=1, source_target_pairs={{0,1},{1,0},{2,3},{3,2},{4,5},{5,4},{6,7},{7,6},{8,9},{9,8},{10,11... | collective-permute-start | bytes 159752 | tf_op jit(solution)/shard_map/ppermute | solution.py:590
  7.0 10.9 %copy-start = (f32[8,3]{0,1:T(4,128)S(1)}, f32[8,3]{0,1:T(4,128)}, u32[]{:S(2)}) copy-start(f32[8,3]{0,1:T(4,128)} %param.7) | copy-start | bytes 292
  7.0 5.9 %collective-permute-start.1 = (f32[104,128]{1,0:T(8,128)S(1)}, f32[104,128]{1,0:T(8,128)S(1)}, u32[]{:S(2)}, u32[]{:S(2)}) collective-permute-start(f32[104,128]{1,0:T(8,128)S(1)} %get-tuple-element.22), channel_id=1, source_target_pairs={{0,3},{1,2},{2,1},{3,0},{4,7},{5,6},{6,5},{7,4},{8,11},{9,10},{10,... | collective-permute-start | bytes 159752 | tf_op jit(solution)/shard_map/ppermute | solution.py:590
  13.3 4.5 %collective-permute-start.3 = (f32[280,128]{1,0:T(8,128)S(1)}, f32[280,128]{1,0:T(8,128)S(1)}, u32[]{:S(2)}, u32[]{:S(2)}) collective-permute-start(f32[280,128]{1,0:T(8,128)S(1)} %get-tuple-element.29), channel_id=1, source_target_pairs={{0,4},{4,0},{8,12},{12,8},{16,20},{20,16},{24,28},{28,24},{1,5},{5... | collective-permute-start | bytes 430088 | tf_op jit(solution)/shard_map/ppermute | solution.py:601
  13.4 4.5 %collective-permute-start.4 = (f32[96,128]{1,0:T(8,128)S(1)}, f32[96,128]{1,0:T(8,128)S(1)}, u32[]{:S(2)}, u32[]{:S(2)}) collective-permute-start(f32[96,128]{1,0:T(8,128)S(1)} %get-tuple-element.30), channel_id=1, source_target_pairs={{0,28},{4,8},{8,4},{12,16},{16,12},{20,24},{24,20},{28,0},{1,29},{... | collective-permute-start | bytes 147464 | tf_op jit(solution)/shard_map/ppermute | solution.py:591
  15.9 4.8 %collective-permute-start.5 = (f32[144,128]{1,0:T(8,128)S(1)}, f32[144,128]{1,0:T(8,128)S(1)}, u32[]{:S(2)}, u32[]{:S(2)}) collective-permute-start(f32[144,128]{1,0:T(8,128)S(1)} %get-tuple-element.34), channel_id=1, source_target_pairs={{0,28},{4,8},{8,4},{12,16},{16,12},{20,24},{24,20},{28,0},{1,29},{... | collective-permute-start | bytes 221192 | tf_op jit(solution)/shard_map/ppermute | solution.py:602
where the time goes:
time: 22.5 us; the launch traced here: 22.3 us
  starting transfers between devices  8.44 us (38%)
  Pallas kernels  8.34 us (37%)
  waiting for transfers between devices  5.53 us (25%)
    ppermute x3, starting transfers between devices, on_device(): q.append(lax.ppermute(x, 'col', step[0]))  5.68 us
    ppermute x3, waiting for transfers between devices, on_device(): q.append(lax.ppermute(x, 'col', step[0]))  3.62 us
    pallas_call x1, Pallas kernels, on_device(): pl.pallas_call(functools.partial(local_kernel, count, low, where), out_sh...  2.75 us
    ppermute x1, starting transfers between devices, on_device(): far = lax.ppermute(far, 'row', odd_pairs(row_count))  2.55 us
    pallas_call x1, Pallas kernels, on_device(): pl.pallas_call(functools.partial(stage_kernel, count, where, cuts), out_s...  2.29 us
    ppermute x1, waiting for transfers between devices, on_device(): far = lax.ppermute(far, 'row', odd_pairs(row_count))  1.77 us
    pallas_call x1, Pallas kernels, on_device(): pl.pallas_call(functools.partial(main_kernel, count, bands, where), out_s...  1.6 us
    pallas_call x1, Pallas kernels, on_device(): pl.pallas_call(functools.partial(pack_kernel, count, where), out_shape=[V...  1.31 us
  transfers between devices with their start and end apart: 6, of which 4 were waited for; matrix products, arithmetic and copies ran while one was open for 0% of the time, Pallas kernels for 23%

commit v1 on v0

--- a/solution.py
+++ b/solution.py
@@ -373,19 +373,6 @@
     )
 
 
-def columns(x, cols, table, level):
-    half = cols // 2
-    high = x.shape[0]
-    wide = 2 * COEFS + REACH
-    main = rows3(split(jnp.concatenate([x[:, :half], x[:, half:cols]], 0)), table.two(f"c1{level}"))
-    out = []
-    for h in range(2):
-        rim = split(x[:, cols + h * 128 : cols + h * 128 + wide])
-        product = dot3 if high % 16 else rows3
-        out.append(main[h * high : (h + 1) * high] + product(rim, table.two(f"c2{level}{h}")))
-    return out
-
-
 def low_columns(x_ref, y_ref, table):
     x = split(x_ref[:, 0 : 128 + 2 * RIM])
     half = y_ref.shape[1] // 2
@@ -453,10 +440,21 @@
     wide = 2 * COEFS + REACH
     x = xe[...]
     before = [pan_ref[:, h * half : (h + 1) * half] for h in range(2)]
+    levels = lambda name: tuple(
+        jnp.concatenate([table.two(name(level))[k] for level in range(LEVELS)], 1) for k in range(2)
+    )
+    high_x = 2 * COEFS
+    main_z = rows3(split(jnp.concatenate([x[:, :half], x[:, half:cols]], 0)), levels(lambda level: f"c1{level}"))
+    zs = [
+        main_z[h * high_x : (h + 1) * high_x]
+        + rows3(split(x[:, cols + h * 128 : cols + h * 128 + wide]), levels(lambda level: f"c2{level}{h}"))
+        for h in range(2)
+    ]
     for level in range(LEVELS):
         ohi, olo = table.pair(f"own{level}")
         t = dot(jnp.concatenate([ohi, ohi], 1), both) + dot(olo, hi)
-        for h, z in enumerate(columns(x, cols, table, level)):
+        for h in range(2):
+            z = zs[h][:, level * half : (level + 1) * half]
             hs = slice(h * half, (h + 1) * half)
             de = dot(table[f"edge{level}"], three_high(z))
             e = e1[level, :, hs] + rows3(split(t[:, h * 128 : h * 128 + wide]), table.two(f"c2{level}{h}"))

time: 22.5 us -> 22.5 us (level)
  transfers between devices with their start and end apart: 6 -> 6, of which waited for: 4 -> 4; matrix products, arithmetic and copies ran while one was open for 0% -> 0% of each run, Pallas kernels for 23% -> 22%
where the time goes in v1:
time: 22.5 us; the launch traced here: 22.3 us
  starting transfers between devices  8.44 us (38%)
  Pallas kernels  8.26 us (37%)
  waiting for transfers between devices  5.56 us (25%)
    ppermute x3, starting transfers between devices, on_device(): q.append(lax.ppermute(x, 'col', step[0]))  5.68 us
    ppermute x3, waiting for transfers between devices, on_device(): q.append(lax.ppermute(x, 'col', step[0]))  3.62 us
    pallas_call x1, Pallas kernels, on_device(): pl.pallas_call(functools.partial(local_kernel, count, low, where), out_sh...  2.71 us
    ppermute x1, starting transfers between devices, on_device(): far = lax.ppermute(far, 'row', odd_pairs(row_count))  2.55 us
    pallas_call x1, Pallas kernels, on_device(): pl.pallas_call(functools.partial(stage_kernel, count, where, cuts), out_s...  2.29 us
    ppermute x1, waiting for transfers between devices, on_device(): far = lax.ppermute(far, 'row', odd_pairs(row_count))  1.77 us
    pallas_call x1, Pallas kernels, on_device(): pl.pallas_call(functools.partial(main_kernel, count, bands, where), out_s...  1.57 us
    pallas_call x1, Pallas kernels, on_device(): pl.pallas_call(functools.partial(pack_kernel, count, where), out_shape=[V...  1.31 us
  transfers between devices with their start and end apart: 6, of which 4 were waited for; matrix products, arithmetic and copies ran while one was open for 0% of the time, Pallas kernels for 22%

profile of v1, /device:TPU:0, one launch (start us, length us, event | category | flops | bytes accessed | tf_op | source)
XLA Modules:
  0.0 22.3 jit_solution(11110078150215859576)
XLA Ops:
  0.0 1.3 %pack.1 = (f32[104,128]{1,0:T(8,128)S(1)}, f32[104,128]{1,0:T(8,128)S(1)}, f32[80,128]{1,0:T(8,128)S(1)}, f32[96,128]{1,0:T(8,128)S(1)}) custom-call(f32[2,32,512]{2,1,0:T(8,128)} %ms_ref.1, f32[128,512]{1,0:T(8,128)} %pan_ref.1, bf16[64,256]{1,0:T(8,128)(2,1)} %constant.4.clone.table_ref), custom_call_target="tpu_custom_call" | custom-call | tf_op jit(solution)/shard_map/pack/pallas_call | solution.py:553
  1.3 4.1 %collective-permute-start.2 = (f32[80,128]{1,0:T(8,128)S(1)}, f32[80,128]{1,0:T(8,128)S(1)}, u32[]{:S(2)}, u32[]{:S(2)}) collective-permute-start(f32[80,128]{1,0:T(8,128)S(1)} %get-tuple-element.23), channel_id=1, source_target_pairs={{0,2},{1,3},{2,0},{3,1},{4,6},{5,7},{6,4},{7,5},{8,10},{9,11},{10,... | collective-permute-start | bytes 122888 | tf_op jit(solution)/shard_map/ppermute | solution.py:588
  5.4 1.6 %collective-permute-start = (f32[104,128]{1,0:T(8,128)S(1)}, f32[104,128]{1,0:T(8,128)S(1)}, u32[]{:S(2)}, u32[]{:S(2)}) collective-permute-start(f32[104,128]{1,0:T(8,128)S(1)} %get-tuple-element.21), channel_id=1, source_target_pairs={{0,1},{1,0},{2,3},{3,2},{4,5},{5,4},{6,7},{7,6},{8,9},{9,8},{10,11... | collective-permute-start | bytes 159752 | tf_op jit(solution)/shard_map/ppermute | solution.py:588
  7.0 0.0 copy-start
  7.0 0.0 collective-permute-start.1
  7.0 2.3 %stage.1 = (f32[80,128]{1,0:T(8,128)S(1)}, f32[96,128]{1,0:T(8,128)S(1)}, f32[96,128]{1,0:T(8,128)S(1)}, f32[128,512]{1,0:T(8,128)S(1)}, bf16[4704,256]{1,0:T(8,128)(2,1)S(1)}, /*index=5*/f32[3,128,512]{2,1,0:T(8,128)S(1)}) custom-call(f32[2,32,512]{2,1,0:T(8,128)} %ms_ref.1, f32[128,512]{1,0:T(8,128)} %pan_ref.1, bf16[4704,256]{1,0:T(8,128)(2,1)} %constant.5.clone.refs_2_), custom_call_target="tpu_custom_call" | custom-call | flops 1000000000 | bytes 1000000 | tf_op jit(solution)/shard_map/stage/pallas_call | solution.py:569
  9.3 0.0 collective-permute-done.2.refs_3_
  9.3 0.2 %collective-permute-done.refs_1_ = f32[104,128]{1,0:T(8,128)S(1)} collective-permute-done((f32[104,128]{1,0:T(8,128)S(1)}, f32[104,128]{1,0:T(8,128)S(1)}, u32[]{:S(2)}, u32[]{:S(2)}) %collective-permute-start) | collective-permute-done | bytes 53280 | tf_op jit(solution)/shard_map/ppermute | solution.py:588
  9.5 3.4 %collective-permute-done.1.refs_2_ = f32[104,128]{1,0:T(8,128)S(1)} collective-permute-done((f32[104,128]{1,0:T(8,128)S(1)}, f32[104,128]{1,0:T(8,128)S(1)}, u32[]{:S(2)}, u32[]{:S(2)}) %collective-permute-start.1) | collective-permute-done | bytes 53280 | tf_op jit(solution)/shard_map/ppermute | solution.py:588
  12.9 0.4 %rim.1 = (f32[280,128]{1,0:T(8,128)S(1)}, f32[144,128]{1,0:T(8,128)S(1)}, f32[128,128]{1,0:T(8,128)S(1)}) custom-call(f32[96,128]{1,0:T(8,128)S(1)} %get-tuple-element.25.top_ref, f32[96,128]{1,0:T(8,128)S(1)} %get-tuple-element.26.bot_ref, bf16[4704,256]{1,0:T(8,128)(2,1)S(1)} %get-tuple-element.27.table_ref.refs_9_.refs_3_, ...), custom_call_target="tpu_custom_call" | custom-call | tf_op jit(solution)/shard_map/rim/pallas_call | solution.py:591
  13.3 0.0 collective-permute-start.3
  13.4 2.5 %collective-permute-start.4 = (f32[96,128]{1,0:T(8,128)S(1)}, f32[96,128]{1,0:T(8,128)S(1)}, u32[]{:S(2)}, u32[]{:S(2)}) collective-permute-start(f32[96,128]{1,0:T(8,128)S(1)} %get-tuple-element.30), channel_id=1, source_target_pairs={{0,28},{4,8},{8,4},{12,16},{16,12},{20,24},{24,20},{28,0},{1,29},{... | collective-permute-start | bytes 147464 | tf_op jit(solution)/shard_map/ppermute | solution.py:589
  15.9 0.2 collective-permute-start.5
  16.1 1.8 %collective-permute-done.4.refs_7_ = f32[96,128]{1,0:T(8,128)S(1)} collective-permute-done((f32[96,128]{1,0:T(8,128)S(1)}, f32[96,128]{1,0:T(8,128)S(1)}, u32[]{:S(2)}, u32[]{:S(2)}) %collective-permute-start.4) | collective-permute-done | bytes 49184 | tf_op jit(solution)/shard_map/ppermute | solution.py:589
  17.8 0.0 collective-permute-done.3.refs_6_
  17.8 0.0 copy-done
  17.9 2.7 %local.1 = (f32[8,128,512]{2,1,0:T(8,128)S(1)}, f32[448,216]{1,0:T(8,128)S(1)}) custom-call(f32[3,8]{1,0:T(4,128)S(1)} %bitcast.1, f32[80,128]{1,0:T(8,128)S(1)} %get-tuple-element.20.refs_0_, f32[104,128]{1,0:T(8,128)S(1)} %collective-permute-done.refs_1_, f32[104,128]{1,0:T(8,128)S(1)} %collective-permute-done.1.refs_2_, ...), custom_call_target="tpu_custom_call" | custom-call | flops 4000000000 | bytes 1000000 | tf_op jit(solution)/shard_map/local/pallas_call | solution.py:602
  20.6 0.2 collective-permute-done.5.refs_2_
  20.7 1.6 %combine.1 = f32[8,128,512]{2,1,0:T(8,128)} custom-call(f32[8,128,512]{2,1,0:T(8,128)S(1)} %get-tuple-element.32.refs_0_, f32[448,216]{1,0:T(8,128)S(1)} %get-tuple-element.33.refs_1_, f32[144,128]{1,0:T(8,128)S(1)} %collective-permute-done.5.refs_2_, bf16[4704,256]{1,0:T(8,128)(2,1)S(1)} %get-tuple-element.27.table_ref.refs_9_.refs_3_), custom_call_target="tpu_custom_call" | custom-call | tf_op jit(solution)/shard_map/combine/pallas_call | solution.py:621
Async XLA Ops:
  1.3 8.0 %collective-permute-start.2 = (f32[80,128]{1,0:T(8,128)S(1)}, f32[80,128]{1,0:T(8,128)S(1)}, u32[]{:S(2)}, u32[]{:S(2)}) collective-permute-start(f32[80,128]{1,0:T(8,128)S(1)} %get-tuple-element.23), channel_id=1, source_target_pairs={{0,2},{1,3},{2,0},{3,1},{4,6},{5,7},{6,4},{7,5},{8,10},{9,11},{10,... | collective-permute-start | bytes 122888 | tf_op jit(solution)/shard_map/ppermute | solution.py:588
  5.4 4.1 %collective-permute-start = (f32[104,128]{1,0:T(8,128)S(1)}, f32[104,128]{1,0:T(8,128)S(1)}, u32[]{:S(2)}, u32[]{:S(2)}) collective-permute-start(f32[104,128]{1,0:T(8,128)S(1)} %get-tuple-element.21), channel_id=1, source_target_pairs={{0,1},{1,0},{2,3},{3,2},{4,5},{5,4},{6,7},{7,6},{8,9},{9,8},{10,11... | collective-permute-start | bytes 159752 | tf_op jit(solution)/shard_map/ppermute | solution.py:588
  7.0 10.9 %copy-start = (f32[8,3]{0,1:T(4,128)S(1)}, f32[8,3]{0,1:T(4,128)}, u32[]{:S(2)}) copy-start(f32[8,3]{0,1:T(4,128)} %param.7) | copy-start | bytes 292
  7.0 5.9 %collective-permute-start.1 = (f32[104,128]{1,0:T(8,128)S(1)}, f32[104,128]{1,0:T(8,128)S(1)}, u32[]{:S(2)}, u32[]{:S(2)}) collective-permute-start(f32[104,128]{1,0:T(8,128)S(1)} %get-tuple-element.22), channel_id=1, source_target_pairs={{0,3},{1,2},{2,1},{3,0},{4,7},{5,6},{6,5},{7,4},{8,11},{9,10},{10,... | collective-permute-start | bytes 159752 | tf_op jit(solution)/shard_map/ppermute | solution.py:588
  13.3 4.5 %collective-permute-start.3 = (f32[280,128]{1,0:T(8,128)S(1)}, f32[280,128]{1,0:T(8,128)S(1)}, u32[]{:S(2)}, u32[]{:S(2)}) collective-permute-start(f32[280,128]{1,0:T(8,128)S(1)} %get-tuple-element.29), channel_id=1, source_target_pairs={{0,4},{4,0},{8,12},{12,8},{16,20},{20,16},{24,28},{28,24},{1,5},{5... | collective-permute-start | bytes 430088 | tf_op jit(solution)/shard_map/ppermute | solution.py:599
  13.4 4.5 %collective-permute-start.4 = (f32[96,128]{1,0:T(8,128)S(1)}, f32[96,128]{1,0:T(8,128)S(1)}, u32[]{:S(2)}, u32[]{:S(2)}) collective-permute-start(f32[96,128]{1,0:T(8,128)S(1)} %get-tuple-element.30), channel_id=1, source_target_pairs={{0,28},{4,8},{8,4},{12,16},{16,12},{20,24},{24,20},{28,0},{1,29},{... | collective-permute-start | bytes 147464 | tf_op jit(solution)/shard_map/ppermute | solution.py:589
  15.9 4.8 %collective-permute-start.5 = (f32[144,128]{1,0:T(8,128)S(1)}, f32[144,128]{1,0:T(8,128)S(1)}, u32[]{:S(2)}, u32[]{:S(2)}) collective-permute-start(f32[144,128]{1,0:T(8,128)S(1)} %get-tuple-element.34), channel_id=1, source_target_pairs={{0,28},{4,8},{8,4},{12,16},{16,12},{20,24},{24,20},{28,0},{1,29},{... | collective-permute-start | bytes 221192 | tf_op jit(solution)/shard_map/ppermute | solution.py:600
